TPU v7x, 128 devices: a whole 4x4x4 slice. The times are simulated.
128 devices in a mesh: date: 8 (over y, z_lo), space: 16 (over x, z_hi, core).
Axes of the slice: x: 4, y: 4, z: 4 (z_hi: 2, z_lo: 2; z = z_hi * 2 + z_lo), core: 2. Of those that a mesh axis runs over, the one named last changes fastest.
Arguments:
- acquisitions: bfloat16 [2, 128, 384, 2304], P(None, 'date', 'space'), may hold values from -6 to 6
- valid_dates: int32 [128, 384, 2304], P('date', 'space'), may hold values 0 or 1
Outputs:
- linked: float32 [2, 128, 64, 768], P(None, 'date', 'space')
All inputs are finite; a program needn't handle non-finite values. No bound on the sum of `valid_dates` on one device may be relied on, other than what follows from the above.
Results may differ from a plain program's by a relative error of at most 0.0028.
Values may be sent and summed in bfloat16 or wider, within the bound.
A program may use at most 256 MiB of HBM per device.

v0:
```python
import jax
import jax.numpy as jnp
from jax import lax
from jax.sharding import PartitionSpec as P

BOX_ROWS = 15
BOX_COLS = 7
STEP_ROWS = 3
STEP_COLS = 6
ITERS = 4
MARGIN = 6
NBOX = 105


POWER_EPS = 1e-05


def padded(block, sides, width):
    for axis, dim in sides:
        count = lax.axis_size(axis)
        forward = [(i, i + 1) for i in range(count - 1)]
        backward = [(target, source) for source, target in forward]
        low = lax.ppermute(
            lax.slice_in_dim(block, block.shape[dim] - width, None, axis=dim), axis, forward
        )
        high = lax.ppermute(lax.slice_in_dim(block, 0, width, axis=dim), axis, backward)
        block = jnp.concatenate([low, block, high], axis=dim)
    return block


def regroup(outgoing):
    return lax.all_to_all(outgoing, ("date", "space"), split_axis=0, concat_axis=0, tiled=True)


def link_all(framed, all_dates, out_cols, row_groups):
    span = STEP_COLS * (out_cols - 1) + 1

    def link_row(out_row):
        band_rows = lax.dynamic_slice_in_dim(framed, out_row * STEP_ROWS, BOX_ROWS, 2)
        window = jnp.stack(
            [band_rows[..., k : k + span : STEP_COLS] for k in range(BOX_COLS)], axis=3
        )
        real_sum = jnp.einsum(
            "adrkc,aerkc->cde", window, window, preferred_element_type=jnp.float32
        )
        cross_sum = jnp.einsum(
            "drkc,erkc->cde", window[1], window[0], preferred_element_type=jnp.float32
        )
        energy = jnp.diagonal(real_sum, axis1=1, axis2=2) / NBOX + POWER_EPS
        factor = lax.rsqrt(energy)
        weights = factor[:, :, None] * factor[:, None, :] / NBOX
        coh_real = (real_sum * weights).astype(jnp.bfloat16)
        coh_imag = ((cross_sum - jnp.swapaxes(cross_sum, 1, 2)) * weights).astype(jnp.bfloat16)
        vec_real = jnp.ones((out_cols, all_dates), jnp.bfloat16)
        vec_imag = jnp.zeros((out_cols, all_dates), jnp.bfloat16)
        real_out = jnp.zeros((out_cols, all_dates), jnp.float32)
        imag_out = jnp.zeros((out_cols, all_dates), jnp.float32)
        for sweep in range(ITERS):
            real_out = jnp.einsum(
                "cde,ce->cd", coh_real, vec_real, preferred_element_type=jnp.float32
            ) - jnp.einsum("cde,ce->cd", coh_imag, vec_imag, preferred_element_type=jnp.float32)
            imag_out = jnp.einsum(
                "cde,ce->cd", coh_imag, vec_real, preferred_element_type=jnp.float32
            ) + jnp.einsum("cde,ce->cd", coh_real, vec_imag, preferred_element_type=jnp.float32)
            total = (
                jnp.sum(real_out * real_out + imag_out * imag_out, axis=1) / all_dates + POWER_EPS
            )
            norm_factor = lax.rsqrt(total)[:, None]
            real_out = real_out * norm_factor
            imag_out = imag_out * norm_factor
            vec_real = real_out.astype(jnp.bfloat16)
            vec_imag = imag_out.astype(jnp.bfloat16)
        return jnp.stack([real_out, imag_out])

    return lax.map(link_row, jnp.arange(row_groups, dtype=jnp.int32))


def on_device(acquisitions, valid_dates):
    date_count = lax.axis_size("date")
    space_count = lax.axis_size("space")
    tile_count = date_count * space_count
    masked = acquisitions * valid_dates.astype(jnp.bfloat16)[None]
    local_dates = masked.shape[1]
    local_cols = masked.shape[2]
    strip_rows = masked.shape[3]
    all_dates = date_count * local_dates
    left_pad = STEP_COLS // 2
    tile_rows = strip_rows // tile_count
    middle = masked.reshape(2, local_dates, local_cols, tile_count, tile_rows)
    outgoing = jnp.transpose(middle, (3, 0, 1, 4, 2))
    incoming = regroup(outgoing)
    height = incoming.shape[3]
    stacked = incoming.reshape(date_count, space_count, 2, local_dates, height, local_cols)
    stacked = jnp.transpose(stacked, (2, 0, 3, 4, 1, 5)).reshape(
        2, all_dates, height, space_count * local_cols
    )
    extended = padded(stacked, ((("date", "space"), 2),), MARGIN)
    total_cols = space_count * local_cols
    framed = jnp.pad(extended, ((0, 0), (0, 0), (0, 0), (left_pad, BOX_COLS - STEP_COLS)))
    out_cols = total_cols // STEP_COLS
    row_groups = tile_rows // STEP_ROWS
    rows_out = link_all(framed, all_dates, out_cols, row_groups)
    col_share = out_cols // space_count
    sending = rows_out.reshape(row_groups, 2, space_count, col_share, date_count, local_dates)
    sending = jnp.transpose(sending, (4, 2, 1, 5, 0, 3)).reshape(
        tile_count, 2, local_dates, row_groups, col_share
    )
    returned = lax.all_to_all(sending, ("date", "space"), split_axis=0, concat_axis=0, tiled=True)
    linked = jnp.transpose(returned, (1, 2, 4, 0, 3)).reshape(
        2, local_dates, col_share, tile_count * row_groups
    )
    return linked


def solution(mesh):
    in_specs = (P(None, "date", "space", None), P("date", "space", None))
    out_specs = P(None, "date", "space", None)
    return jax.shard_map(
        on_device, mesh=mesh, in_specs=in_specs, out_specs=out_specs, check_vma=False
    )
```

profile of v0, /device:TPU:1, one launch (start us, length us, event | category | flops | bytes accessed | tf_op | source)
XLA Modules:
  0.0 713.2 jit_solution(16303320604601856355)
XLA Ops:
  3.4 61.6 %reshape.51 = bf16[2,16,24,128,18]{4,3,2,1,0:T(8,128)(2,1)} reshape(bf16[2,16,24,2304]{3,2,1,0:T(8,128)(2,1)S(1)} %broadcast_multiply_fusion) | data formatting | bytes 7077888 | tf_op jit(solution)/shard_map/reshape | solution.py:89
  65.1 40.3 %copy.56 = bf16[128,2,16,18,24]{4,2,3,1,0:T(8,128)(2,1)} copy(bf16[128,2,16,18,24]{3,0,4,2,1:T(8,128)(2,1)} %bitcast.252) | data formatting | bytes 7077888 | tf_op jit(solution)/shard_map/transpose | solution.py:90
  105.3 28.7 %reshape.89 = bf16[128,2,6912]{2,1,0:T(2,128)(2,1)S(1)} reshape(bf16[128,2,18,16,24]{4,3,2,1,0:T(8,128)(2,1)} %bitcast.254) | data formatting | bytes 7077888
  134.1 56.8 %all_to_all.10 = bf16[128,2,6912]{2,1,0:T(2,128)(2,1)} all-to-all(bf16[128,2,6912]{2,1,0:T(2,128)(2,1)S(1)} %reshape.89), channel_id=1, replica_groups=mesh['date'=8,'space'=16] {'date','space'}, dimensions={0} | all-to-all | bytes 7077888 | tf_op jit(solution)/shard_map/all_to_all | solution.py:32
  190.8 33.8 %reshape.90 = bf16[128,2,18,16,24]{4,3,2,1,0:T(8,128)(2,1)} reshape(bf16[128,2,6912]{2,1,0:T(2,128)(2,1)} %all_to_all.10) | data formatting | bytes 7077888
  224.7 31.5 %copy.58 = bf16[2,8,16,18,16,24]{5,4,2,1,3,0:T(8,128)(2,1)} copy(bf16[2,8,16,18,16,24]{5,2,3,0,4,1:T(8,128)(2,1)} %bitcast.253) | data formatting | bytes 7077888 | tf_op jit(solution)/shard_map/transpose | solution.py:94
  256.2 23.6 %reshape.53 = bf16[2,128,18,384]{3,1,2,0:T(8,128)(2,1)S(1)} reshape(bf16[2,8,16,18,16,24]{5,4,2,1,3,0:T(8,128)(2,1)} %copy.58) | data formatting | bytes 7077888 | tf_op jit(solution)/shard_map/reshape | solution.py:94
  288.0 24.1 %collective-permute-done = bf16[2,128,6,384]{3,1,2,0:T(8,128)(2,1)} collective-permute-done((bf16[2,128,6,384]{3,1,2,0:T(8,128)(2,1)}, bf16[2,128,6,384]{3,1,2,0:T(8,128)(2,1)}, u32[]{:S(2)}, u32[]{:S(2)}) %collective-permute-start) | collective-permute-done | bytes 1179680 | tf_op jit(solution)/shard_map/ppermute | solution.py:23
  312.2 4.9 pad_maximum_fusion
  317.1 9.1 %copy.91 = bf16[2,128,30,384]{1,2,3,0:T(8,128)(2,1)} copy(bf16[2,128,30,384]{3,1,2,0:T(8,128)(2,1)} %pad_maximum_fusion) | data formatting | bytes 11796480
  326.1 6.7 pad.4.clone
  332.8 346.1 %while.10 = (s32[]{:T(128)}, f32[6,2,64,128]{3,2,1,0:T(8,128)S(1)}, s32[6]{0:T(128)S(1)}, bf16[2,128,30,388]{1,2,3,0:T(8,128)(2,1)}, s32[]{:T(128)}, /*index=5*/s32[1]{0:T(128)}, s32[]{:T(128)}, s32[]{:T(128)}) while((s32[]{:T(128)}, f32[6,2,64,128]{3,2,1,0:T(8,128)S(1)}, s32[6]{0:T(128)S(1)}, bf16[2,128,30,388]{1,2,3,0:T(8,128)(2,1)}, ...), condition=%wide.region_5.6_spmd, body=%wide.region_0.5_spmd.sunk | while | flops 701842176 | bytes 111707832 | solution.py:75
  354.6 7.0 copy.144
  368.3 5.6 copy.143
  373.9 5.6 fusion.153
  410.5 7.0 copy.144
  424.1 5.6 copy.143
  429.7 5.6 fusion.153
  466.3 7.0 copy.144
  475.1 4.8 convolution_bitcast_fusion.4
  480.0 5.6 copy.143
  485.6 5.6 fusion.153
  522.2 7.0 copy.144
  535.8 5.6 copy.143
  541.4 5.6 fusion.153
  578.0 7.0 copy.144
  591.7 5.6 copy.143
  597.3 5.6 fusion.153
  633.9 7.0 copy.144
  647.5 5.6 copy.143
  653.1 5.6 fusion.153
  686.2 19.3 %all_to_all.11 = f32[128,1,768]{2,1,0:T(1,128)S(1)} all-to-all(f32[128,1,768]{2,1,0:T(1,128)S(1)} %reshape.91), channel_id=1, replica_groups=mesh['date'=8,'space'=16] {'date','space'}, dimensions={0} | all-to-all | bytes 786432 | tf_op jit(solution)/shard_map/all_to_all | solution.py:108
  (296 shorter events, 242.7 us)
Async XLA Ops:
  0.0 3.1 copy-start
  281.5 30.7 %collective-permute-start = (bf16[2,128,6,384]{3,1,2,0:T(8,128)(2,1)}, bf16[2,128,6,384]{3,1,2,0:T(8,128)(2,1)}, u32[]{:S(2)}, u32[]{:S(2)}) collective-permute-start(bf16[2,128,6,384]{3,1,2,0:T(8,128)(2,1)} %get-tuple-element.70), channel_id=1, source_target_pairs={{0,1},{1,2},{2,3},{3,4},{4,5},{5,6},{6,7},{7,8},{8,9},{9,10},{10,1... | collective-permute-start | bytes 3538952 | tf_op jit(solution)/shard_map/ppermute | solution.py:23
  286.1 26.1 %collective-permute-start.1 = (bf16[2,128,6,384]{3,1,2,0:T(8,128)(2,1)}, bf16[2,128,6,384]{3,1,2,0:T(8,128)(2,1)}, u32[]{:S(2)}, u32[]{:S(2)}) collective-permute-start(bf16[2,128,6,384]{3,1,2,0:T(8,128)(2,1)} %get-tuple-element.71), channel_id=1, source_target_pairs={{1,0},{2,1},{3,2},{4,3},{5,4},{6,5},{7,6},{8,7},{9,8},{10,9},{11,1... | collective-permute-start | bytes 3538952 | tf_op jit(solution)/shard_map/ppermute | solution.py:26
  326.1 6.7 copy-start.2
  349.3 1.9 copy-start.1
  405.1 1.9 copy-start.1
  461.0 1.9 copy-start.1
  516.8 1.9 copy-start.1
  572.7 1.9 copy-start.1
  628.5 1.9 copy-start.1
where the time goes:
time: 721 us; the launch traced here: 713 us
  local copies, waits for them, and re-layouts  378 us (52%)
  matrix products  164 us (23%)
  blocking collectives  76 us (11%)
  other arithmetic  47.9 us (7%)
  waiting for transfers between devices  24.1 us (3%)
  loops' own time  16 us (2%)
    unnamed x9, local copies, waits for them, and re-layouts  78.5 us
    reshape x1, local copies, waits for them, and re-layouts, on_device(): middle = masked.reshape(2, local_dates, local_cols, tile_count, tile_rows)  61.6 us
    all_to_all x1, blocking collectives, regroup(): lax.all_to_all(outgoing, ('date', 'space'), split_axis=0, concat_axis=0,...  56.8 us
    dot_general x6, local copies, waits for them, and re-layouts, link_row(): jnp.einsum('adrkc,aerkc->cde', window, window, preferred_element_type=jnp...  41.8 us
    transpose x1, local copies, waits for them, and re-layouts, on_device(): outgoing = jnp.transpose(middle, (3, 0, 1, 4, 2))  40.3 us
    dot_general x6, local copies, waits for them, and re-layouts, link_row(): jnp.einsum('drkc,erkc->cde', window[1], window[0], preferred_element_type...  33.6 us
    convert_element_type x6, other arithmetic, link_row(): ((cross_sum - jnp.swapaxes(cross_sum, 1, 2)) * weights).astype(jnp.bfloat16)  33.5 us
    transpose x1, local copies, waits for them, and re-layouts, on_device(): jnp.transpose(stacked, (2, 0, 3, 4, 1, 5))  31.5 us
  transfers between devices with their start and end apart: 2, of which 1 were waited for; matrix products, arithmetic and copies ran while one was open for 0% of the time, Pallas kernels for 0%

commit v1 on v0

v1 whole, which is shorter than its diff:
```python
import jax
import jax.numpy as jnp
from jax import lax
from jax.experimental import pallas as pl
from jax.experimental.pallas import tpu as pltpu
from jax.sharding import PartitionSpec as P

MESH = pl.DeviceIdType.MESH
EPS = 1e-05
NBOX = 105
NDATE = 8
NSPACE = 16
LD = 16
LC = 24
ROWS = 2304
WIN = 96
WIDE = 256
TAIL = 44
TILES = ROWS // 128 + 2

CHUNKS = (
    (4, 9, (0, 4), 4, ((8, 0, 5),)),
    (9, 16, (4, 10), 9, ((15, 5, 5),)),
    (16, 24, (10, 16), 16, ((22, 10, 5), (23, 15, 5))),
    (24, 31, (16, 22), 24, ((30, 20, 2),)),
)
BLOCKS = 31


def block_of(col):
    if col < 0:
        return col + 3
    for first, _, (low, high), start, _ in CHUNKS:
        if low <= col < high:
            return start + col - low


def tails_of(out_col):
    low, high = 6 * out_col - 3, 6 * out_col + 3
    found = []
    for block, first, count in [(3, -3, 3)] + [t for ch in CHUNKS for t in ch[4]]:
        start, stop = max(low, first), min(high, first + count - 1)
        if start <= stop:
            found.append((block, start - first, stop - first))
    return found


def dot(left, right):
    return lax.dot_general(
        left, right, (((1,), (0,)), ((), ())), preferred_element_type=jnp.float32
    )


def dot_t(left, right):
    return lax.dot_general(
        left, right, (((1,), (1,)), ((), ())), preferred_element_type=jnp.float32
    )


def split(value):
    high = value.astype(jnp.bfloat16)
    low = (value - high.astype(jnp.float32)).astype(jnp.bfloat16)
    return high, low


def kernel(
    acq_hbm, val_hbm, out_ref,
    acq, val, masked, send, recv, squares, band, back, home,
    in_sem, send_sem, recv_sem, side_send, side_recv, own_sem,
    back_send, back_recv, back_own,
):
    me = lax.axis_index("date")
    strip = lax.axis_index("space")
    right = lax.rem(strip + 1, NSPACE)
    left = lax.rem(strip + NSPACE - 1, NSPACE)
    my_rows = pl.ds(pl.multiple_of(me * LD, LD), LD)

    def load(octet):
        cols = pl.ds(8 * octet, 8)
        return (
            pltpu.make_async_copy(
                acq_hbm.at[:, :, cols, :], acq.at[:, :, cols, :], in_sem.at[0, octet]
            ),
            pltpu.make_async_copy(
                val_hbm.at[:, cols, :], val.at[:, cols, :], in_sem.at[1, octet]
            ),
        )

    for octet in (2, 0, 1):
        for copy in load(octet):
            copy.start()

    barrier = pltpu.get_barrier_semaphore()
    for hop in range(1, NDATE):
        pl.semaphore_signal(
            barrier, inc=1, device_id=(lax.rem(me + hop, NDATE), strip), device_id_type=MESH
        )
    for hop in range(NDATE):
        pl.semaphore_signal(
            barrier, inc=1, device_id=(lax.rem(me + hop, NDATE), left), device_id_type=MESH
        )

    row = lax.broadcasted_iota(jnp.int32, (2 * WIN, WIDE), 0)
    lane = lax.broadcasted_iota(jnp.int32, (2 * WIN, WIDE), 1)
    row = jnp.where(row >= WIN, row - WIN, row)
    band[...] = jnp.where((lane >= 3 * row) & (lane <= 3 * row + 14), 1.0, 0.0)

    masked[0] = jnp.zeros((2 * LD * LC, 128), jnp.float32)
    masked[TILES - 1] = jnp.zeros((2 * LD * LC, 128), jnp.float32)

    def mask(octet):
        for copy in load(octet):
            copy.wait()

        def body(date, carry):
            cols = pl.ds(8 * octet, 8)
            valid = val[date, cols, :].astype(jnp.float32)
            for part in range(2):
                value = acq[part, date, cols, :].astype(jnp.float32) * valid
                at = pl.multiple_of(part * (LD * LC) + date * LC + 8 * octet, 8)
                for tile in range(TILES - 2):
                    masked[1 + tile, pl.ds(at, 8), :] = value[:, tile * 128 : tile * 128 + 128]
            return carry

        lax.fori_loop(0, LD, body, 0)

    def strip_tiles(part, col, tile, count):
        at = pl.ds(part * (LD * LC) + col, LD, stride=LC)
        return jnp.concatenate([masked[tile + j, at, :] for j in range(count)], axis=1)

    def pack_main(low, high, start):
        def body(step, carry):
            col = low + step // 2
            part = step % 2
            block = start + step // 2
            for k in range(NDATE):
                at = 122 + 288 * k
                tile, shift = at // 128, at % 128
                value = strip_tiles(part, col, tile, 3)
                send[k, block, part] = value[:, shift : shift + WIDE].astype(jnp.bfloat16)
            return carry

        lax.fori_loop(0, 2 * (high - low), body, 0)

    def pack_tail(block, first, count):
        place = lax.broadcasted_iota(jnp.int32, (LD, WIDE), 1)

        def body(part, carry):
            for k in range(NDATE):
                at = 122 + 288 * k + WIDE
                tile, shift = at // 128, at % 128
                total = jnp.zeros((LD, WIDE), jnp.float32)
                for q in range(count):
                    value = strip_tiles(part, first + q, tile, 2)
                    moved = pltpu.roll(value, (TAIL * q - shift) % WIDE, 1)
                    here = (place >= TAIL * q) & (place < TAIL * (q + 1))
                    total = jnp.where(here, moved, total)
                send[k, block, part] = total.astype(jnp.bfloat16)
            return carry

        lax.fori_loop(0, 2, body, 0)

    def own_copy(chunk, hop):
        low, high = CHUNKS[chunk][:2]
        to = lax.rem(me + hop, NDATE)
        return pltpu.make_async_remote_copy(
            src_ref=send.at[to, low:high],
            dst_ref=recv.at[low:high, :, my_rows],
            send_sem=send_sem.at[chunk, hop],
            recv_sem=recv_sem.at[chunk, hop],
            device_id=(to, strip),
            device_id_type=MESH,
        )

    def own_local(chunk):
        low, high = CHUNKS[chunk][:2]
        return pltpu.make_async_copy(
            send.at[me, low:high], recv.at[low:high, :, my_rows], own_sem.at[chunk]
        )

    def side_copy(hop):
        to = lax.rem(me + hop, NDATE)
        return pltpu.make_async_remote_copy(
            src_ref=send.at[to, 0:4],
            dst_ref=recv.at[0:4, :, my_rows],
            send_sem=side_send.at[hop],
            recv_sem=side_recv.at[hop],
            device_id=(to, right),
            device_id_type=MESH,
        )

    def back_copy(out_col, hop):
        to = lax.rem(me + hop, NDATE)
        rows = pl.ds(pl.multiple_of(to * LD, LD), LD)
        return pltpu.make_async_remote_copy(
            src_ref=back.at[out_col, :, rows],
            dst_ref=home.at[me, out_col],
            send_sem=back_send.at[out_col, hop],
            recv_sem=back_recv.at[out_col, hop],
            device_id=(to, strip),
            device_id_type=MESH,
        )

    def back_local(out_col):
        return pltpu.make_async_copy(
            back.at[out_col, :, my_rows], home.at[me, out_col], back_own.at[out_col]
        )

    mask(2)
    pack_main(21, 24, 0)
    pack_tail(3, 21, 3)
    pl.semaphore_wait(barrier, 2 * NDATE - 1)
    for hop in range(NDATE):
        side_copy(hop).start()
    mask(0)
    for chunk, (_, _, (low, high), start, tails) in enumerate(CHUNKS):
        if chunk == 1:
            mask(1)
        pack_main(low, high, start)
        for tail in tails:
            pack_tail(*tail)
        for hop in range(1, NDATE):
            own_copy(chunk, hop).start()
        own_local(chunk).start()

    def pixels(block):
        return recv[block].reshape(2 * 128, WIDE)

    def tail_band(low, high):
        row = lax.broadcasted_iota(jnp.int32, (16, WIDE), 0) + (WIN - 16)
        lane = lax.broadcasted_iota(jnp.int32, (16, WIDE), 1)
        at = lane - TAIL * low
        for q in range(low + 1, high + 1):
            at = jnp.where(lane >= TAIL * q, lane - TAIL * q, at)
        at = at + WIDE
        inside = (lane >= TAIL * low) & (lane < TAIL * (high + 1))
        return jnp.where(inside & (at >= 3 * row) & (at <= 3 * row + 14), 1.0, 0.0)

    def link(out_col):
        mains = [block_of(col) for col in range(6 * out_col - 3, 6 * out_col + 4)]
        tails = [(block, tail_band(low, high)) for block, low, high in tails_of(out_col)]

        for at in range(0, 2 * 128, 32):
            part, date = at // 128, at % 128
            total = jnp.zeros((32, WIDE), jnp.float32)
            for block in mains:
                value = recv[block, part, date : date + 32, :].astype(jnp.float32)
                total = total + value * value
            high, low = split(total)
            squares[0, at : at + 32, :] = high
            squares[1, at : at + 32, :] = low
        ones = band[0:WIN, :].astype(jnp.bfloat16)
        power = dot_t(ones, squares[0]) + dot_t(ones, squares[1])
        more = jnp.zeros((16, 2 * 128), jnp.float32)
        for block, mask_ in tails:
            value = pixels(block).astype(jnp.float32)
            high, low = split(value * value)
            ones = mask_.astype(jnp.bfloat16)
            more = more + dot_t(ones, high) + dot_t(ones, low)
        power = jnp.concatenate([power[: WIN - 16], power[WIN - 16 :] + more], axis=0)
        energy = (power[:, :128] + power[:, 128:]) / NBOX + EPS
        factor = lax.rsqrt(energy)

        def sweep(step, vector):
            real, imag = vector
            real, imag = real * factor, imag * factor
            wide = jnp.concatenate(
                [
                    jnp.concatenate([real, imag], axis=1),
                    jnp.concatenate([imag, -real], axis=1),
                ],
                axis=0,
            )
            high, low = split(wide)
            total = jnp.zeros((2 * WIN, 2 * 128), jnp.float32)
            for block in mains:
                matrix = pixels(block)
                seen = (dot(high, matrix) + dot(low, matrix)) * band[...]
                seen_high, seen_low = split(seen)
                total = total + (dot_t(seen_high, matrix) + dot_t(seen_low, matrix))
            last = lambda x: jnp.concatenate([x[WIN - 16 : WIN], x[2 * WIN - 16 :]], axis=0)
            high, low = last(high), last(low)
            more = jnp.zeros((32, 2 * 128), jnp.float32)
            for block, mask_ in tails:
                matrix = pixels(block)
                seen = (dot(high, matrix) + dot(low, matrix)) * jnp.concatenate([mask_, mask_], 0)
                seen_high, seen_low = split(seen)
                more = more + (dot_t(seen_high, matrix) + dot_t(seen_low, matrix))
            first = jnp.concatenate([total[: WIN - 16], total[WIN - 16 : WIN] + more[:16]], axis=0)
            second = jnp.concatenate(
                [total[WIN : 2 * WIN - 16], total[2 * WIN - 16 :] + more[16:]], axis=0
            )
            scale = factor * (1.0 / NBOX)
            real = (first[:, :128] - second[:, 128:]) * scale
            imag = (first[:, 128:] + second[:, :128]) * scale
            size = jnp.sum(real * real + imag * imag, axis=1, keepdims=True) / 128 + EPS
            norm = lax.rsqrt(size)
            return real * norm, imag * norm

        start = (jnp.ones((WIN, 128), jnp.float32), jnp.zeros((WIN, 128), jnp.float32))
        real, imag = lax.fori_loop(0, 4, sweep, start)
        fill = jnp.zeros((128 - WIN, 128), jnp.float32)
        back[out_col, 0] = jnp.concatenate([real, fill], axis=0).T
        back[out_col, 1] = jnp.concatenate([imag, fill], axis=0).T

    for out_col in range(4):
        if out_col == 0:
            for hop in range(NDATE):
                side_copy(hop).wait_recv()

            @pl.when(strip == 0)
            def _():
                recv[0:4] = jnp.zeros((4, 2, 128, WIDE), jnp.bfloat16)

        for hop in range(1, NDATE):
            own_copy(out_col, hop).wait_recv()
        own_local(out_col).wait()
        link(out_col)
        for hop in range(1, NDATE):
            back_copy(out_col, hop).start()
        back_local(out_col).start()

    place = lax.broadcasted_iota(jnp.int32, (LD, 128), 1)
    for out_col in range(4):
        for hop in range(1, NDATE):
            back_copy(out_col, hop).wait_recv()
        back_local(out_col).wait()
        for part in range(2):
            for tile in range(6):
                k, at = tile * 128 // WIN, tile * 128 % WIN
                value = pltpu.roll(home[k, out_col, part], (-at) % 128, 1)
                done = WIN - at
                while done < 128:
                    k += 1
                    more = home[k, out_col, part]
                    if done:
                        more = pltpu.roll(more, done, 1)
                    value = jnp.where(place < done, value, more)
                    done += WIN
                out_ref[tile, pl.ds(part * (LD * 4) + out_col, LD, stride=4), :] = value

    for chunk in range(4):
        for hop in range(1, NDATE):
            own_copy(chunk, hop).wait_send()
            back_copy(chunk, hop).wait_send()
    for hop in range(NDATE):
        side_copy(hop).wait_send()


def on_device(acquisitions, valid_dates):
    dma = pltpu.SemaphoreType.DMA
    out = pl.pallas_call(
        kernel,
        name="link_phases",
        out_shape=jax.ShapeDtypeStruct((6, 2 * LD * 4, 128), jnp.float32),
        in_specs=[pl.BlockSpec(memory_space=pl.ANY)] * 2,
        out_specs=pl.BlockSpec(memory_space=pltpu.VMEM),
        scratch_shapes=[
            pltpu.VMEM((2, LD, LC, ROWS), jnp.bfloat16),
            pltpu.VMEM((LD, LC, ROWS), jnp.int32),
            pltpu.VMEM((TILES, 2 * LD * LC, 128), jnp.float32),
            pltpu.VMEM((NDATE, BLOCKS, 2, LD, WIDE), jnp.bfloat16),
            pltpu.VMEM((BLOCKS, 2, 128, WIDE), jnp.bfloat16),
            pltpu.VMEM((2, 2 * 128, WIDE), jnp.bfloat16),
            pltpu.VMEM((2 * WIN, WIDE), jnp.float32),
            pltpu.VMEM((4, 2, 128, 128), jnp.float32),
            pltpu.VMEM((NDATE, 4, 2, LD, 128), jnp.float32),
            dma((2, 3)),
            dma((4, NDATE)),
            dma((4, NDATE)),
            dma((NDATE,)),
            dma((NDATE,)),
            dma((4,)),
            dma((4, NDATE)),
            dma((4, NDATE)),
            dma((4,)),
        ],
        compiler_params=pltpu.CompilerParams(
            collective_id=0, has_side_effects=True, vmem_limit_bytes=56 << 20
        ),
    )(acquisitions, valid_dates)
    return jnp.transpose(out, (1, 0, 2)).reshape(2, LD, 4, 768)


def solution(mesh):
    in_specs = (P(None, "date", "space", None), P("date", "space", None))
    out_specs = P(None, "date", "space", None)
    return jax.shard_map(
        on_device, mesh=mesh, in_specs=in_specs, out_specs=out_specs, check_vma=False
    )
```

time: 721 us -> 73.7 us (0.10); the launches traced: 713 us -> 73.6 us
  local copies, waits for them, and re-layouts: 378 us -> 2.14 us
  matrix products: 164 us -> 0 us
  blocking collectives: 76 us -> 0 us
  Pallas kernels: 0 us -> 71.4 us
  other arithmetic: 47.9 us -> 0 us
  waiting for transfers between devices: 24.1 us -> 0 us
  loops' own time: 16 us -> 0 us
    dot_general x108 -> x0, matrix products: 164 us -> none  [the longest x6 29 us: link_row(): jnp.einsum('drkc,erkc->cde', window[1], window[0], preferred_element_type...]
    reshape x5 -> x1, local copies, waits for them, and re-layouts: 90.7 us -> 0.9 us  [on_device(): return jnp.transpose(out, (1, 0, 2)).reshape(2, LD, 4, 768)]
    unnamed x9 -> x0, local copies, waits for them, and re-layouts: 78.5 us -> none
    all_to_all x2 -> x0, blocking collectives: 76 us -> none  [the longest x1 56.8 us: regroup(): lax.all_to_all(outgoing, ('date', 'space'), split_axis=0, concat_axis=0,...]
    dot_general x12 -> x0, local copies, waits for them, and re-layouts: 75.3 us -> none  [the longest x6 41.8 us: link_row(): jnp.einsum('adrkc,aerkc->cde', window, window, preferred_element_type=jnp...]
    transpose x4 -> x1, local copies, waits for them, and re-layouts: 72.9 us -> 1.24 us  [on_device(): return jnp.transpose(out, (1, 0, 2)).reshape(2, LD, 4, 768)]
    pallas_call x0 -> x1, Pallas kernels: none -> 71.4 us  [on_device(): pl.pallas_call(kernel, name='link_phases', out_shape=jax.ShapeDtypeStruct...]
    convert_element_type x25 -> x0, other arithmetic: 37.2 us -> none  [the longest x6 33.5 us: link_row(): ((cross_sum - jnp.swapaxes(cross_sum, 1, 2)) * weights).astype(jnp.bfloat16)]
  transfers between devices with their start and end apart: 2 -> 0, of which waited for: 1 -> 0; matrix products, arithmetic and copies ran while one was open for 0% -> 0% of each run, Pallas kernels for 0% -> 0%
where the time goes in v1:
time: 73.7 us; the launch traced here: 73.6 us
  Pallas kernels  71.4 us (97%)
  local copies, waits for them, and re-layouts  2.14 us (3%)
    pallas_call x1, Pallas kernels, on_device(): pl.pallas_call(kernel, name='link_phases', out_shape=jax.ShapeDtypeStruct...  71.4 us

profile of v1, /device:TPU:1, one launch (start us, length us, event | category | flops | bytes accessed | tf_op | source)
XLA Modules:
  0.0 73.6 jit_solution(4801184899035801068)
XLA Ops:
  0.0 71.4 %link_phases.1 = f32[6,128,128]{2,1,0:T(8,128)} custom-call(bf16[2,16,24,2304]{3,2,1,0:T(8,128)(2,1)} %acq_hbm.1, s32[16,24,2304]{2,1,0:T(8,128)} %val_hbm.1), custom_call_target="tpu_custom_call" | custom-call | tf_op jit(solution)/shard_map/link_phases/pallas_call | solution.py:352
  71.5 1.2 %copy.3 = f32[128,6,128]{2,1,0:T(8,128)S(1)} copy(f32[128,6,128]{2,0,1:T(8,128)} %bitcast.1) | data formatting | bytes 786432 | tf_op jit(solution)/shard_map/transpose | solution.py:382
  72.7 0.9 %reshape.3 = f32[2,16,4,768]{3,2,1,0:T(4,128)} reshape(f32[128,6,128]{2,1,0:T(8,128)S(1)} %copy.3) | data formatting | bytes 786432 | tf_op jit(solution)/shard_map/reshape | solution.py:382

commit v2 on v1

v2 whole, which is shorter than its diff:
```python
import jax
import jax.numpy as jnp
from jax import lax
from jax.experimental import pallas as pl
from jax.experimental.pallas import tpu as pltpu
from jax.sharding import PartitionSpec as P

MESH = pl.DeviceIdType.MESH
EPS = 1e-05
NBOX = 105
NDATE = 8
NSPACE = 16
LD = 16
LC = 24
ROWS = 2304
WIN = 96
WIDE = 256
NEAR = 48
FAR = 64
LAST = 16
TAIL = 44
TILES = ROWS // 128 + 2

CHUNKS = (
    (4, 9, (0, 4), 8, 0),
    (9, 16, (4, 10), 15, 1),
    (16, 23, (10, 16), 22, 2),
    (23, 30, (16, 22), 29, 3),
)
BLOCKS = 30
USED = 22
PEERS = ((3, 1), (1, 0), (2, 1), (3, 0), (0, 1), (2, 0), (1, 1))


def block_of(col):
    if col < 0:
        return col + 3
    for first, _, (low, high), _, _ in CHUNKS:
        if low <= col < high:
            return first + col - low


def tails_of(out_col):
    low, high = 6 * out_col - 3, 6 * out_col + 3
    found = []
    if low < 0:
        found.append((3, 0, low + 3, 2))
    low = max(low, 0)
    for _, _, _, block, place in CHUNKS:
        if TAIL * low < WIDE * (place + 1) and TAIL * (high + 1) > WIDE * place:
            found.append((block, WIDE * place, low, high))
    return found


def dot(left, right):
    return lax.dot_general(
        left, right, (((1,), (0,)), ((), ())), preferred_element_type=jnp.float32
    )


def dot_t(left, right):
    return lax.dot_general(
        left, right, (((1,), (1,)), ((), ())), preferred_element_type=jnp.float32
    )


def split(value):
    high = value.astype(jnp.bfloat16)
    low = (value - high.astype(jnp.float32)).astype(jnp.bfloat16)
    return high, low


def kernel(
    acq_hbm, val_hbm, out_ref,
    acq, val, masked, send, recv, squares, near, far, linked, back, home,
    in_sem, send_sem, recv_sem, side_send, side_recv, own_sem,
    back_send, back_recv, back_own,
):
    me = lax.axis_index("date")
    strip = lax.axis_index("space")
    right = lax.rem(strip + 1, NSPACE)
    left = lax.rem(strip + NSPACE - 1, NSPACE)
    my_rows = pl.ds(pl.multiple_of(me * LD, LD), LD)

    def load(octet):
        cols = pl.ds(8 * octet, 8)
        return (
            pltpu.make_async_copy(
                acq_hbm.at[:, :, cols, :], acq.at[:, :, cols, :], in_sem.at[0, octet]
            ),
            pltpu.make_async_copy(
                val_hbm.at[:, cols, :], val.at[:, cols, :], in_sem.at[1, octet]
            ),
        )

    for octet in (2, 0, 1):
        for copy in load(octet):
            copy.start()

    barrier = pltpu.get_barrier_semaphore()
    for hop in range(1, NDATE):
        pl.semaphore_signal(
            barrier, inc=1, device_id=(lax.rem(me + hop, NDATE), strip), device_id_type=MESH
        )
    for hop in range(NDATE):
        pl.semaphore_signal(
            barrier, inc=1, device_id=(lax.rem(me + hop, NDATE), left), device_id_type=MESH
        )

    def inside(windows, first, rows):
        shape = (2 * windows, 128)
        row = lax.broadcasted_iota(jnp.int32, shape, 0)
        row = jnp.where(row >= windows, row - windows, row) + first
        at = lax.broadcasted_iota(jnp.int32, shape, 1) + rows
        return jnp.where((at >= 3 * row) & (at <= 3 * row + 14), 1.0, 0.0)

    near[...] = inside(NEAR, 0, 0)
    far[...] = inside(FAR, WIN - FAR, 128)

    masked[0] = jnp.zeros((2 * LD * LC, 128), jnp.float32)
    masked[TILES - 1] = jnp.zeros((2 * LD * LC, 128), jnp.float32)

    def mask(octet):
        for copy in load(octet):
            copy.wait()

        def body(date, carry):
            cols = pl.ds(8 * octet, 8)
            valid = val[date, cols, :].astype(jnp.float32)
            for part in range(2):
                value = acq[part, date, cols, :].astype(jnp.float32) * valid
                at = pl.multiple_of(part * (LD * LC) + date * LC + 8 * octet, 8)
                for tile in range(TILES - 2):
                    masked[1 + tile, pl.ds(at, 8), :] = value[:, tile * 128 : tile * 128 + 128]
            return carry

        lax.fori_loop(0, LD, body, 0)

    def strip_tiles(part, col, tile, count):
        at = pl.ds(part * (LD * LC) + col, LD, stride=LC)
        return jnp.concatenate([masked[tile + j, at, :] for j in range(count)], axis=1)

    def pack_main(low, high, start):
        def body(step, carry):
            col = low + step // 2
            part = step % 2
            block = start + step // 2
            for k in range(NDATE):
                at = 122 + 288 * k
                tile, shift = at // 128, at % 128
                value = strip_tiles(part, col, tile, 3)
                send[k, block, part] = value[:, shift : shift + WIDE].astype(jnp.bfloat16)
            return carry

        lax.fori_loop(0, 2 * (high - low), body, 0)

    def pack_tail(block, first, cols):
        place = lax.broadcasted_iota(jnp.int32, (LD, WIDE), 1)

        def body(part, carry):
            for k in range(NDATE):
                at = 122 + 288 * k + WIDE
                tile, shift = at // 128, at % 128
                total = jnp.zeros((LD, WIDE), jnp.float32)
                for q, col in enumerate(cols):
                    start = TAIL * q - first
                    value = strip_tiles(part, col, tile, 2)
                    moved = pltpu.roll(value, (start - shift) % WIDE, 1)
                    here = (place >= start) & (place < start + TAIL)
                    total = jnp.where(here, moved, total)
                send[k, block, part] = total.astype(jnp.bfloat16)
            return carry

        lax.fori_loop(0, 2, body, 0)

    def pack_tails(block, place):
        low, high = WIDE * place // TAIL, min((WIDE * place + WIDE - 1) // TAIL, USED - 1)
        pack_tail(block, WIDE * place - TAIL * low, range(low, high + 1))

    def peer_of(peer):
        along, other = peer
        z = lax.rem(me, 2)
        return 2 * lax.rem(me // 2 + along, NDATE // 2) + (1 - z if other else z)

    def own_copy(chunk, peer):
        low, high = CHUNKS[chunk][:2]
        to = peer_of(peer)
        hop = 2 * peer[0] + peer[1]
        return pltpu.make_async_remote_copy(
            src_ref=send.at[to, low:high],
            dst_ref=recv.at[low:high, :, my_rows],
            send_sem=send_sem.at[chunk, hop],
            recv_sem=recv_sem.at[chunk, hop],
            device_id=(to, strip),
            device_id_type=MESH,
        )

    def own_local(chunk):
        low, high = CHUNKS[chunk][:2]
        return pltpu.make_async_copy(
            send.at[me, low:high], recv.at[low:high, :, my_rows], own_sem.at[chunk]
        )

    def side_copy(hop):
        to = lax.rem(me + hop, NDATE)
        return pltpu.make_async_remote_copy(
            src_ref=send.at[to, 0:4],
            dst_ref=recv.at[0:4, :, my_rows],
            send_sem=side_send.at[hop],
            recv_sem=side_recv.at[hop],
            device_id=(to, right),
            device_id_type=MESH,
        )

    def back_copy(tile, peer):
        to = peer_of(peer)
        hop = 2 * peer[0] + peer[1]
        rows = pl.ds(pl.multiple_of(to * LD, LD), LD)
        return pltpu.make_async_remote_copy(
            src_ref=back.at[tile, :, rows],
            dst_ref=home.at[me, tile],
            send_sem=back_send.at[tile, hop],
            recv_sem=back_recv.at[tile, hop],
            device_id=(to, strip),
            device_id_type=MESH,
        )

    def back_local(tile):
        return pltpu.make_async_copy(
            back.at[tile, :, my_rows], home.at[me, tile], back_own.at[tile]
        )

    mask(2)
    pack_main(21, 24, 0)
    pack_tail(3, 0, (21, 22, 23))
    pl.semaphore_wait(barrier, 2 * NDATE - 1)
    for hop in range(NDATE):
        side_copy(hop).start()
    mask(0)
    for chunk, (start, _, (low, high), block, place) in enumerate(CHUNKS):
        if chunk == 1:
            mask(1)
        pack_main(low, high, start)
        pack_tails(block, place)
        for peer in PEERS:
            own_copy(chunk, peer).start()
        own_local(chunk).start()

    def pixels(block):
        return recv[block].reshape(2 * 128, WIDE)

    def pairs(blocks, lanes):
        one = [recv[block, :, :, lanes : lanes + 128].reshape(2 * 128, 128) for block in blocks]
        return [
            jnp.concatenate(one[j : j + 2], axis=1) if j + 1 < len(one) else one[j]
            for j in range(0, len(one), 2)
        ]

    def tail_band(first, low, high):
        row = lax.broadcasted_iota(jnp.int32, (LAST, WIDE), 0) + (WIN - LAST)
        lane = lax.broadcasted_iota(jnp.int32, (LAST, WIDE), 1) + first
        at = lane - TAIL * low
        for q in range(low + 1, high + 1):
            at = jnp.where(lane >= TAIL * q, lane - TAIL * q, at)
        at = at + WIDE
        here = (lane >= TAIL * low) & (lane < TAIL * (high + 1))
        return jnp.where(here & (at >= 3 * row) & (at <= 3 * row + 14), 1.0, 0.0)

    def merge(first, second, third):
        both = first[WIN - FAR :] + second[: NEAR + FAR - WIN]
        middle = second[NEAR + FAR - WIN : FAR - LAST]
        end = second[FAR - LAST :] + third
        return jnp.concatenate([first[: WIN - FAR], both, middle, end], axis=0)

    def link(out_col):
        mains = [block_of(col) for col in range(6 * out_col - 3, 6 * out_col + 4)]
        tails = [
            (block, tail_band(first, low, high))
            for block, first, low, high in tails_of(out_col)
        ]

        for at in range(0, 2 * 128, 32):
            part, date = at // 128, at % 128
            total = jnp.zeros((32, WIDE), jnp.float32)
            for block in mains:
                value = recv[block, part, date : date + 32, :].astype(jnp.float32)
                total = total + value * value
            high, low = split(total)
            squares[0, at : at + 32, :] = high
            squares[1, at : at + 32, :] = low

        def power(ones, lanes):
            lanes = slice(lanes, lanes + 128)
            return dot_t(ones, squares[0, :, lanes]) + dot_t(ones, squares[1, :, lanes])

        last = jnp.zeros((LAST, 2 * 128), jnp.float32)
        for block, ones in tails:
            value = pixels(block).astype(jnp.float32)
            high, low = split(value * value)
            ones = ones.astype(jnp.bfloat16)
            last = last + dot_t(ones, high) + dot_t(ones, low)
        energy = merge(
            power(near[:NEAR].astype(jnp.bfloat16), 0),
            power(far[:FAR].astype(jnp.bfloat16), 128),
            last,
        )
        energy = (energy[:, :128] + energy[:, 128:]) / NBOX + EPS
        factor = lax.rsqrt(energy)

        def back_and_forth(wide, matrices, bands):
            high, low = split(wide)
            total = None
            for matrix, ones in zip(matrices, bands):
                if ones.shape[1] < matrix.shape[1]:
                    ones = jnp.concatenate([ones, ones], axis=1)
                seen = (dot(high, matrix) + dot(low, matrix)) * ones
                seen_high, seen_low = split(seen)
                more = dot_t(seen_high, matrix) + dot_t(seen_low, matrix)
                total = more if total is None else total + more
            return total

        def sweep(step, vector):
            real, imag = vector
            real, imag = real * factor, imag * factor
            upper = jnp.concatenate([real, imag], axis=1)
            lower = jnp.concatenate([imag, -real], axis=1)
            stack = lambda low, high: jnp.concatenate([upper[low:high], lower[low:high]], axis=0)
            first = back_and_forth(stack(0, NEAR), pairs(mains, 0), [near[...]] * 4)
            second = back_and_forth(stack(WIN - FAR, WIN), pairs(mains, 128), [far[...]] * 4)
            third = back_and_forth(
                stack(WIN - LAST, WIN),
                [pixels(block) for block, _ in tails],
                [jnp.concatenate([ones, ones], axis=0) for _, ones in tails],
            )
            upper = merge(first[:NEAR], second[:FAR], third[:LAST])
            lower = merge(first[NEAR:], second[FAR:], third[LAST:])
            scale = factor * (1.0 / NBOX)
            real = (upper[:, :128] - lower[:, 128:]) * scale
            imag = (upper[:, 128:] + lower[:, :128]) * scale
            size = jnp.sum(real * real + imag * imag, axis=1, keepdims=True) / 128 + EPS
            norm = lax.rsqrt(size)
            return real * norm, imag * norm

        start = (jnp.ones((WIN, 128), jnp.float32), jnp.zeros((WIN, 128), jnp.float32))
        real, imag = lax.fori_loop(0, 4, sweep, start)
        linked[0, out_col * WIN : out_col * WIN + WIN] = real
        linked[1, out_col * WIN : out_col * WIN + WIN] = imag

    def send_back(tile):
        for part in range(2):
            back[tile, part] = linked[part, tile * 128 : tile * 128 + 128].T
        for peer in PEERS:
            back_copy(tile, peer).start()
        back_local(tile).start()

    place = lax.broadcasted_iota(jnp.int32, (LD, 128), 1)

    def assemble(out_col, part, tile):
        value = None
        done = 0
        while done < 128:
            k, window = (tile * 128 + done) // WIN, (tile * 128 + done) % WIN
            source, lane = (out_col * WIN + window) // 128, (out_col * WIN + window) % 128
            more = home[k, source, part]
            if lane != done:
                more = pltpu.roll(more, (done - lane) % 128, 1)
            value = more if value is None else jnp.where(place < done, value, more)
            done += min(WIN - window, 128 - lane, 128 - done)
        out_ref[part, :, out_col, tile * 128 : tile * 128 + 128] = value

    for out_col in range(4):
        if out_col == 0:
            for hop in range(NDATE):
                side_copy(hop).wait_recv()

            @pl.when(strip == 0)
            def _():
                recv[0:4] = jnp.zeros((4, 2, 128, WIDE), jnp.bfloat16)

        for peer in PEERS:
            own_copy(out_col, peer).wait_recv()
        own_local(out_col).wait()
        link(out_col)
        if out_col:
            send_back(out_col - 1)

    for source in range(3):
        for peer in PEERS:
            back_copy(source, peer).wait_recv()
        back_local(source).wait()
        for out_col in ((0,), (1,), (2, 3))[source]:
            for part in range(2):
                for tile in range(6):
                    assemble(out_col, part, tile)

    for peer in PEERS:
        for chunk in range(4):
            own_copy(chunk, peer).wait_send()
        for tile in range(3):
            back_copy(tile, peer).wait_send()
    for hop in range(NDATE):
        side_copy(hop).wait_send()


def on_device(acquisitions, valid_dates):
    dma = pltpu.SemaphoreType.DMA
    return pl.pallas_call(
        kernel,
        name="link_phases",
        out_shape=jax.ShapeDtypeStruct((2, LD, 4, 768), jnp.float32),
        in_specs=[pl.BlockSpec(memory_space=pl.ANY)] * 2,
        out_specs=pl.BlockSpec(memory_space=pltpu.VMEM),
        scratch_shapes=[
            pltpu.VMEM((2, LD, LC, ROWS), jnp.bfloat16),
            pltpu.VMEM((LD, LC, ROWS), jnp.int32),
            pltpu.VMEM((TILES, 2 * LD * LC, 128), jnp.float32),
            pltpu.VMEM((NDATE, BLOCKS, 2, LD, WIDE), jnp.bfloat16),
            pltpu.VMEM((BLOCKS, 2, 128, WIDE), jnp.bfloat16),
            pltpu.VMEM((2, 2 * 128, WIDE), jnp.bfloat16),
            pltpu.VMEM((2 * NEAR, 128), jnp.float32),
            pltpu.VMEM((2 * FAR, 128), jnp.float32),
            pltpu.VMEM((2, 4 * WIN, 128), jnp.float32),
            pltpu.VMEM((3, 2, 128, 128), jnp.float32),
            pltpu.VMEM((NDATE, 3, 2, LD, 128), jnp.float32),
            dma((2, 3)),
            dma((4, NDATE)),
            dma((4, NDATE)),
            dma((NDATE,)),
            dma((NDATE,)),
            dma((4,)),
            dma((3, NDATE)),
            dma((3, NDATE)),
            dma((3,)),
        ],
        compiler_params=pltpu.CompilerParams(
            collective_id=0, has_side_effects=True, vmem_limit_bytes=56 << 20
        ),
    )(acquisitions, valid_dates)


def solution(mesh):
    in_specs = (P(None, "date", "space", None), P("date", "space", None))
    out_specs = P(None, "date", "space", None)
    return jax.shard_map(
        on_device, mesh=mesh, in_specs=in_specs, out_specs=out_specs, check_vma=False
    )
```

time: 73.7 us -> 69.9 us (0.948)
  Pallas kernels: 71.4 us -> 68 us
    pallas_call x1, Pallas kernels: 71.4 us -> 68 us  [on_device(): pl.pallas_call(kernel, name='link_phases', out_shape=jax.ShapeDtypeStruct...]
    unnamed x0 -> x1, local copies, waits for them, and re-layouts: none -> 1.77 us
    transpose x1 -> x0, local copies, waits for them, and re-layouts: 1.24 us -> none  [on_device(): return jnp.transpose(out, (1, 0, 2)).reshape(2, LD, 4, 768)]
    reshape x1 -> x0, local copies, waits for them, and re-layouts: 0.9 us -> none  [on_device(): return jnp.transpose(out, (1, 0, 2)).reshape(2, LD, 4, 768)]
where the time goes in v2:
time: 69.9 us; the launch traced here: 69.8 us
  Pallas kernels  68 us (97%)
  local copies, waits for them, and re-layouts  1.77 us (3%)
    pallas_call x1, Pallas kernels, on_device(): pl.pallas_call(kernel, name='link_phases', out_shape=jax.ShapeDtypeStruct...  68 us
    unnamed x1, local copies, waits for them, and re-layouts  1.77 us

profile of v2, /device:TPU:1, one launch (start us, length us, event | category | flops | bytes accessed | tf_op | source)
XLA Modules:
  0.0 69.8 jit_solution(7629652358420850624)
XLA Ops:
  0.0 68.0 %link_phases.1 = f32[2,16,4,768]{3,2,1,0:T(4,128)} custom-call(bf16[2,16,24,2304]{3,2,1,0:T(8,128)(2,1)} %acq_hbm.1, s32[16,24,2304]{2,1,0:T(8,128)} %val_hbm.1), custom_call_target="tpu_custom_call" | custom-call | tf_op jit(solution)/shard_map/link_phases/pallas_call | solution.py:407
  68.0 1.8 %copy.4 = f32[2,16,4,768]{3,2,1,0:T(4,128)} copy(f32[2,16,4,768]{3,2,1,0:T(4,128)} %link_phases.1) | data formatting | bytes 786432

commit v3 on v2

--- a/solution.py
+++ b/solution.py
@@ -308,16 +308,17 @@
         factor = lax.rsqrt(energy)
 
         def back_and_forth(wide, matrices, bands):
-            high, low = split(wide)
+            count = wide.shape[0]
+            wide = jnp.concatenate(split(wide), axis=0)
             total = None
             for matrix, ones in zip(matrices, bands):
                 if ones.shape[1] < matrix.shape[1]:
                     ones = jnp.concatenate([ones, ones], axis=1)
-                seen = (dot(high, matrix) + dot(low, matrix)) * ones
-                seen_high, seen_low = split(seen)
-                more = dot_t(seen_high, matrix) + dot_t(seen_low, matrix)
+                seen = dot(wide, matrix)
+                seen = (seen[:count] + seen[count:]) * ones
+                more = dot_t(jnp.concatenate(split(seen), axis=0), matrix)
                 total = more if total is None else total + more
-            return total
+            return total[:count] + total[count:]
 
         def sweep(step, vector):
             real, imag = vector

time: 69.9 us -> 66.3 us (0.948)
  Pallas kernels: 68 us -> 64.4 us
    pallas_call x1, Pallas kernels: 68 us -> 64.4 us  [on_device(): pl.pallas_call(kernel, name='link_phases', out_shape=jax.ShapeDtypeStruct...]
where the time goes in v3:
time: 66.3 us; the launch traced here: 66.2 us
  Pallas kernels  64.4 us (97%)
  local copies, waits for them, and re-layouts  1.77 us (3%)
    pallas_call x1, Pallas kernels, on_device(): pl.pallas_call(kernel, name='link_phases', out_shape=jax.ShapeDtypeStruct...  64.4 us
    unnamed x1, local copies, waits for them, and re-layouts  1.77 us

profile of v3, /device:TPU:1, one launch (start us, length us, event | category | flops | bytes accessed | tf_op | source)
XLA Modules:
  0.0 66.2 jit_solution(11802868580020829939)
XLA Ops:
  0.0 64.4 %link_phases.1 = f32[2,16,4,768]{3,2,1,0:T(4,128)} custom-call(bf16[2,16,24,2304]{3,2,1,0:T(8,128)(2,1)} %acq_hbm.1, s32[16,24,2304]{2,1,0:T(8,128)} %val_hbm.1), custom_call_target="tpu_custom_call" | custom-call | tf_op jit(solution)/shard_map/link_phases/pallas_call | solution.py:408
  64.4 1.8 %copy.4 = f32[2,16,4,768]{3,2,1,0:T(4,128)} copy(f32[2,16,4,768]{3,2,1,0:T(4,128)} %link_phases.1) | data formatting | bytes 786432

commit v4 on v3

--- a/solution.py
+++ b/solution.py
@@ -28,8 +28,10 @@
     (23, 30, (16, 22), 29, 3),
 )
 BLOCKS = 30
+CODE = 7.5
 USED = 22
-PEERS = ((3, 1), (1, 0), (2, 1), (3, 0), (0, 1), (2, 0), (1, 1))
+ORDER = 5
+PEERS = range(1, NDATE)
 
 
 def block_of(col):
@@ -93,9 +95,8 @@
             ),
         )
 
-    for octet in (2, 0, 1):
-        for copy in load(octet):
-            copy.start()
+    for copy in load(2):
+        copy.start()
 
     barrier = pltpu.get_barrier_semaphore()
     for hop in range(1, NDATE):
@@ -121,8 +122,9 @@
     masked[TILES - 1] = jnp.zeros((2 * LD * LC, 128), jnp.float32)
 
     def mask(octet):
-        for copy in load(octet):
-            copy.wait()
+        if octet < 2:
+            for copy in load(octet):
+                copy.wait()
 
         def body(date, carry):
             cols = pl.ds(8 * octet, 8)
@@ -136,56 +138,68 @@
 
         lax.fori_loop(0, LD, body, 0)
 
-    def strip_tiles(part, col, tile, count):
+    def hop_of(turn):
+        return lax.rem(ORDER * turn, NDATE)
+
+    def peer_of(turn):
+        hop = hop_of(turn)
+        z = lax.rem(me, 2)
+        return 2 * lax.rem(me // 2 + hop // 2, NDATE // 2) + lax.rem(z + hop, 2)
+
+    def mask_for(octet, k):
+        first = (122 + 288 * k) // 128
+
+        def body(date, carry):
+            cols = pl.ds(8 * octet, 8)
+            for j in range(4):
+                tile = jnp.clip(first + j, 1, TILES - 2)
+                rows = pl.ds(pl.multiple_of((tile - 1) * 128, 128), 128)
+                valid = val[date, cols, rows].astype(jnp.float32)
+                for part in range(2):
+                    value = acq[part, date, cols, rows].astype(jnp.float32) * valid
+                    at = pl.multiple_of(part * (LD * LC) + date * LC + 8 * octet, 8)
+                    masked[tile, pl.ds(at, 8), :] = value
+            return carry
+
+        lax.fori_loop(0, LD, body, 0, unroll=4)
+
+    spot = lax.broadcasted_iota(jnp.int32, (LD, 128), 1)
+
+    def turned(part, col, k, skip, count):
+        first = 122 + 288 * k
+        tile = first // 128
+        rest = 128 - (first - tile * 128)
         at = pl.ds(part * (LD * LC) + col, LD, stride=LC)
-        return jnp.concatenate([masked[tile + j, at, :] for j in range(count)], axis=1)
-
-    def pack_main(low, high, start):
-        def body(step, carry):
-            col = low + step // 2
-            part = step % 2
-            block = start + step // 2
-            for k in range(NDATE):
-                at = 122 + 288 * k
-                tile, shift = at // 128, at % 128
-                value = strip_tiles(part, col, tile, 3)
-                send[k, block, part] = value[:, shift : shift + WIDE].astype(jnp.bfloat16)
-            return carry
-
-        lax.fori_loop(0, 2 * (high - low), body, 0)
-
-    def pack_tail(block, first, cols):
-        place = lax.broadcasted_iota(jnp.int32, (LD, WIDE), 1)
-
-        def body(part, carry):
-            for k in range(NDATE):
-                at = 122 + 288 * k + WIDE
-                tile, shift = at // 128, at % 128
-                total = jnp.zeros((LD, WIDE), jnp.float32)
-                for q, col in enumerate(cols):
-                    start = TAIL * q - first
-                    value = strip_tiles(part, col, tile, 2)
-                    moved = pltpu.roll(value, (start - shift) % WIDE, 1)
-                    here = (place >= start) & (place < start + TAIL)
-                    total = jnp.where(here, moved, total)
-                send[k, block, part] = total.astype(jnp.bfloat16)
-            return carry
-
-        lax.fori_loop(0, 2, body, 0)
-
-    def pack_tails(block, place):
+        raw = [pltpu.roll(masked[tile + skip + j, at, :], rest, 1) for j in range(count + 1)]
+        return [jnp.where(spot < rest, raw[j], raw[j + 1]) for j in range(count)]
+
+    def pack_main(k, low, high, start):
+        for col in range(low, high):
+            for part in range(2):
+                value = jnp.concatenate(turned(part, col, k, 0, 2), axis=1)
+                send[k, start + col - low, part] = value.astype(jnp.bfloat16)
+
+    def pack_tail(k, block, first, cols):
+        for part in range(2):
+            halves = [jnp.zeros((LD, 128), jnp.float32)] * 2
+            for q, col in enumerate(cols):
+                value = turned(part, col, k, 2, 1)[0]
+                for half in range(2):
+                    start = TAIL * q - first - 128 * half
+                    if -TAIL < start < 128:
+                        moved = pltpu.roll(value, start % 128, 1) if start % 128 else value
+                        here = (spot >= start) & (spot < start + TAIL)
+                        halves[half] = jnp.where(here, moved, halves[half])
+            send[k, block, part] = jnp.concatenate(halves, axis=1).astype(jnp.bfloat16)
+
+    def pack_tails(k, block, place):
         low, high = WIDE * place // TAIL, min((WIDE * place + WIDE - 1) // TAIL, USED - 1)
-        pack_tail(block, WIDE * place - TAIL * low, range(low, high + 1))
-
-    def peer_of(peer):
-        along, other = peer
-        z = lax.rem(me, 2)
-        return 2 * lax.rem(me // 2 + along, NDATE // 2) + (1 - z if other else z)
+        pack_tail(k, block, WIDE * place - TAIL * low, range(low, high + 1))
 
     def own_copy(chunk, peer):
         low, high = CHUNKS[chunk][:2]
         to = peer_of(peer)
-        hop = 2 * peer[0] + peer[1]
+        hop = hop_of(peer)
         return pltpu.make_async_remote_copy(
             src_ref=send.at[to, low:high],
             dst_ref=recv.at[low:high, :, my_rows],
@@ -201,8 +215,9 @@
             send.at[me, low:high], recv.at[low:high, :, my_rows], own_sem.at[chunk]
         )
 
-    def side_copy(hop):
-        to = lax.rem(me + hop, NDATE)
+    def side_copy(peer):
+        to = peer_of(peer)
+        hop = hop_of(peer)
         return pltpu.make_async_remote_copy(
             src_ref=send.at[to, 0:4],
             dst_ref=recv.at[0:4, :, my_rows],
@@ -214,7 +229,7 @@
 
     def back_copy(tile, peer):
         to = peer_of(peer)
-        hop = 2 * peer[0] + peer[1]
+        hop = hop_of(peer)
         rows = pl.ds(pl.multiple_of(to * LD, LD), LD)
         return pltpu.make_async_remote_copy(
             src_ref=back.at[tile, :, rows],
@@ -230,20 +245,45 @@
             back.at[tile, :, my_rows], home.at[me, tile], back_own.at[tile]
         )
 
+    for copy in load(2):
+        copy.wait()
+    for octet in range(2):
+        for copy in load(octet):
+            copy.start()
+
+    def fill_side(turn):
+        to = peer_of(turn)
+        pack_main(to, 21, 24, 0)
+        pack_tail(to, 3, 0, (21, 22, 23))
+
+    def send_side(turn, carry):
+        fill_side(turn)
+        side_copy(turn).start()
+        return carry
+
+    mask_for(2, peer_of(1))
+    fill_side(1)
+    pl.semaphore_wait(barrier, 2 * NDATE - 1)
+    side_copy(1).start()
     mask(2)
-    pack_main(21, 24, 0)
-    pack_tail(3, 0, (21, 22, 23))
-    pl.semaphore_wait(barrier, 2 * NDATE - 1)
-    for hop in range(NDATE):
-        side_copy(hop).start()
+    lax.fori_loop(2, NDATE + 1, send_side, 0)
     mask(0)
     for chunk, (start, _, (low, high), block, place) in enumerate(CHUNKS):
         if chunk == 1:
             mask(1)
-        pack_main(low, high, start)
-        pack_tails(block, place)
-        for peer in PEERS:
-            own_copy(chunk, peer).start()
+
+        def send_own(turn, carry):
+            to = peer_of(turn)
+            pack_main(to, low, high, start)
+            pack_tails(to, block, place)
+
+            @pl.when(turn < NDATE)
+            def _():
+                own_copy(chunk, turn).start()
+
+            return carry
+
+        lax.fori_loop(1, NDATE + 1, send_own, 0)
         own_local(chunk).start()
 
     def pixels(block):
@@ -343,13 +383,14 @@
             return real * norm, imag * norm
 
         start = (jnp.ones((WIN, 128), jnp.float32), jnp.zeros((WIN, 128), jnp.float32))
-        real, imag = lax.fori_loop(0, 4, sweep, start)
+        real, imag = lax.fori_loop(0, 4, sweep, start, unroll=True)
         linked[0, out_col * WIN : out_col * WIN + WIN] = real
         linked[1, out_col * WIN : out_col * WIN + WIN] = imag
 
     def send_back(tile):
         for part in range(2):
-            back[tile, part] = linked[part, tile * 128 : tile * 128 + 128].T
+            value = linked[part, tile * 128 : tile * 128 + 128].T
+            back[tile, part] = jnp.exp(value * CODE).astype(jnp.bfloat16)
         for peer in PEERS:
             back_copy(tile, peer).start()
         back_local(tile).start()
@@ -362,7 +403,7 @@
         while done < 128:
             k, window = (tile * 128 + done) // WIN, (tile * 128 + done) % WIN
             source, lane = (out_col * WIN + window) // 128, (out_col * WIN + window) % 128
-            more = home[k, source, part]
+            more = jnp.log(home[k, source, part].astype(jnp.float32)) * (1.0 / CODE)
             if lane != done:
                 more = pltpu.roll(more, (done - lane) % 128, 1)
             value = more if value is None else jnp.where(place < done, value, more)
@@ -371,8 +412,8 @@
 
     for out_col in range(4):
         if out_col == 0:
-            for hop in range(NDATE):
-                side_copy(hop).wait_recv()
+            for peer in range(1, NDATE + 1):
+                side_copy(peer).wait_recv()
 
             @pl.when(strip == 0)
             def _():
@@ -399,8 +440,8 @@
             own_copy(chunk, peer).wait_send()
         for tile in range(3):
             back_copy(tile, peer).wait_send()
-    for hop in range(NDATE):
-        side_copy(hop).wait_send()
+    for peer in range(1, NDATE + 1):
+        side_copy(peer).wait_send()
 
 
 def on_device(acquisitions, valid_dates):
@@ -421,8 +462,8 @@
             pltpu.VMEM((2 * NEAR, 128), jnp.float32),
             pltpu.VMEM((2 * FAR, 128), jnp.float32),
             pltpu.VMEM((2, 4 * WIN, 128), jnp.float32),
-            pltpu.VMEM((3, 2, 128, 128), jnp.float32),
-            pltpu.VMEM((NDATE, 3, 2, LD, 128), jnp.float32),
+            pltpu.VMEM((3, 2, 128, 128), jnp.bfloat16),
+            pltpu.VMEM((NDATE, 3, 2, LD, 128), jnp.bfloat16),
             dma((2, 3)),
             dma((4, NDATE)),
             dma((4, NDATE)),

time: 66.3 us -> 63.4 us (0.956)
  Pallas kernels: 64.4 us -> 61.4 us
    pallas_call x1, Pallas kernels: 64.4 us -> 61.4 us  [on_device(): pl.pallas_call(kernel, name='link_phases', out_shape=jax.ShapeDtypeStruct...]
where the time goes in v4:
time: 63.4 us; the launch traced here: 63.2 us
  Pallas kernels  61.4 us (97%)
  local copies, waits for them, and re-layouts  1.77 us (3%)
    pallas_call x1, Pallas kernels, on_device(): pl.pallas_call(kernel, name='link_phases', out_shape=jax.ShapeDtypeStruct...  61.4 us
    unnamed x1, local copies, waits for them, and re-layouts  1.77 us

profile of v4, /device:TPU:1, one launch (start us, length us, event | category | flops | bytes accessed | tf_op | source)
XLA Modules:
  0.0 63.2 jit_solution(13509332991735511829)
XLA Ops:
  0.0 61.4 %link_phases.1 = f32[2,16,4,768]{3,2,1,0:T(4,128)} custom-call(bf16[2,16,24,2304]{3,2,1,0:T(8,128)(2,1)} %acq_hbm.1, s32[16,24,2304]{2,1,0:T(8,128)} %val_hbm.1), custom_call_target="tpu_custom_call" | custom-call | tf_op jit(solution)/shard_map/link_phases/pallas_call | solution.py:449
  61.4 1.8 %copy.4 = f32[2,16,4,768]{3,2,1,0:T(4,128)} copy(f32[2,16,4,768]{3,2,1,0:T(4,128)} %link_phases.1) | data formatting | bytes 786432

commit v5 on v4

--- a/solution.py
+++ b/solution.py
@@ -30,7 +30,7 @@
 BLOCKS = 30
 CODE = 7.5
 USED = 22
-ORDER = 5
+ORDER = 7917224
 PEERS = range(1, NDATE)
 
 
@@ -139,7 +139,9 @@
         lax.fori_loop(0, LD, body, 0)
 
     def hop_of(turn):
-        return lax.rem(ORDER * turn, NDATE)
+        hop = (ORDER >> (3 * turn)) & 7
+        mirrored = lax.rem(NDATE - hop // 2 * 2, NDATE) + lax.rem(hop, 2)
+        return jnp.where(lax.rem(me // 2, 2) == 1, mirrored, hop)
 
     def peer_of(turn):
         hop = hop_of(turn)

time: 63.4 us -> 63.1 us (level)
  no operation moved by 1% of the time
where the time goes in v5:
time: 63.1 us; the launch traced here: 62.9 us
  Pallas kernels  61.2 us (97%)
  local copies, waits for them, and re-layouts  1.77 us (3%)
    pallas_call x1, Pallas kernels, on_device(): pl.pallas_call(kernel, name='link_phases', out_shape=jax.ShapeDtypeStruct...  61.2 us
    unnamed x1, local copies, waits for them, and re-layouts  1.77 us

profile of v5, /device:TPU:1, one launch (start us, length us, event | category | flops | bytes accessed | tf_op | source)
XLA Modules:
  0.0 62.9 jit_solution(8121850679461949927)
XLA Ops:
  0.0 61.2 %link_phases.1 = f32[2,16,4,768]{3,2,1,0:T(4,128)} custom-call(bf16[2,16,24,2304]{3,2,1,0:T(8,128)(2,1)} %acq_hbm.1, s32[16,24,2304]{2,1,0:T(8,128)} %val_hbm.1), custom_call_target="tpu_custom_call" | custom-call | tf_op jit(solution)/shard_map/link_phases/pallas_call | solution.py:451
  61.2 1.8 %copy.4 = f32[2,16,4,768]{3,2,1,0:T(4,128)} copy(f32[2,16,4,768]{3,2,1,0:T(4,128)} %link_phases.1) | data formatting | bytes 786432
